TPU v7x, 32 devices: a whole 2x2x4 slice. The times are simulated.
32 devices in a mesh: rep: 2 (over x), exp: 2 (over core), tp: 8 (over z, y).
Axes of the slice: x: 2, y: 2, z: 4, core: 2. Of those that a mesh axis runs over, the one named last changes fastest.
Arguments:
- tokens: bfloat16 [128, 4096], P(('rep', 'exp', 'tp')), parts along dimension 0, may hold values from -6 to 6
- expert_ids: int32 [128, 2], P(('rep', 'exp', 'tp')), parts along dimension 0, may hold values from 0 to 3, all different within a row; in each aligned block of 4 rows (0 to 3, 4 to 7, ...) at most 4 rows name the same one
- gate_ints: int32 [128, 2], P(('rep', 'exp', 'tp')), parts along dimension 0, may hold values from 16 to 240, as said below
- gate_weight: bfloat16 [4, 4096, 14336], P('exp', None, 'tp'), may hold values from -0.09375 to 0.09375
- up_weight: bfloat16 [4, 4096, 14336], P('exp', None, 'tp'), may hold values from -0.09375 to 0.09375
- down_weight: bfloat16 [4, 14336, 4096], P('exp', 'tp'), may hold values from -0.046875 to 0.046875
Outputs:
- mixed: bfloat16 [128, 4096], P(('rep', 'exp', 'tp')), parts along dimension 0
There are 2 independent parts, one for each index of `rep`. A program takes and returns all parts, laid end to end along the dimension named above; an argument that names none is the same for every part. Nothing has to cross between parts.
Inputs may be any that keep to these rules, and one draw needn't show every extreme that they name: `expert_ids`: each row names two different experts. Among the 4 rows of one device an expert is named at most 4 times, and exactly that often on some device. `gate_ints`: the two entries of a row sum to 256.
All inputs are finite; a program needn't handle non-finite values.
Results may differ from a plain program's by a relative error of at most 0.0049.
Values may be sent and summed in bfloat16 or wider, within the bound.
A program may use at most 128 MiB of HBM per device.

v0:
```python
import jax
import jax.numpy as jnp
from jax import lax
from jax.sharding import PartitionSpec as P


def body(tokens, expert_ids, gate_ints, gate_weight, up_weight, down_weight):
    tok_rows, width = tokens.shape
    local_experts = gate_weight.shape[0]
    groups = lax.axis_size("exp")
    experts_all = local_experts * groups
    columns = experts_all * tok_rows
    flat_ids = expert_ids.reshape(-1)
    onehot = (flat_ids[:, None] == jnp.arange(experts_all, dtype=jnp.int32)[None, :]).astype(
        jnp.int32
    )
    before = jnp.cumsum(onehot, axis=0) - onehot
    position = jnp.sum(before * onehot, axis=1)
    owner = flat_ids // local_experts
    local = flat_ids % local_experts
    send_index = flat_ids * tok_rows + position
    placing = (send_index[:, None] == jnp.arange(columns, dtype=jnp.int32)[None, :]).astype(
        jnp.float32
    )
    placing = placing.reshape(tok_rows, 2, columns).sum(axis=1).astype(jnp.bfloat16)
    outgoing = jnp.einsum("tm,td->md", placing, tokens, preferred_element_type=jnp.float32).astype(
        jnp.bfloat16
    )
    outgoing = outgoing.reshape(groups, local_experts, tok_rows, width)
    arrived = lax.all_to_all(outgoing, "exp", split_axis=0, concat_axis=2, tiled=True)
    arrived = arrived.reshape(local_experts, groups * tok_rows, width)
    piece = lax.all_gather(arrived, "tp", axis=1, tiled=True)
    gate = jnp.einsum("lrd,ldf->lrf", piece, gate_weight, preferred_element_type=jnp.float32)
    upper = jnp.einsum("lrd,ldf->lrf", piece, up_weight, preferred_element_type=jnp.float32)
    hidden = (jax.nn.silu(gate) * upper).astype(jnp.bfloat16)
    summed = lax.psum_scatter(
        jnp.einsum("lrf,lfd->rld", hidden, down_weight, preferred_element_type=jnp.float32),
        "tp",
        scatter_dimension=0,
        tiled=True,
    )
    summed = summed.reshape(groups, tok_rows, local_experts, width)
    back = lax.all_to_all(summed, "exp", split_axis=0, concat_axis=0, tiled=True)
    back_index = (owner * tok_rows + position) * local_experts + local
    gates = gate_ints.reshape(-1).astype(jnp.float32) / 256.0
    combine = jnp.where(
        back_index[:, None] == jnp.arange(columns, dtype=jnp.int32)[None, :], gates[:, None], 0.0
    )
    combine = combine.reshape(tok_rows, 2, columns).sum(axis=1)
    mixed = jnp.dot(
        combine,
        back.reshape(columns, width),
        precision=lax.Precision.HIGHEST,
        preferred_element_type=jnp.float32,
    ).astype(jnp.bfloat16)
    return mixed


def solution(mesh):
    return jax.shard_map(
        body,
        mesh=mesh,
        in_specs=(
            P(("rep", "exp", "tp"), None),
            P(("rep", "exp", "tp"), None),
            P(("rep", "exp", "tp"), None),
            P("exp", None, "tp"),
            P("exp", None, "tp"),
            P("exp", "tp", None),
        ),
        out_specs=P(("rep", "exp", "tp"), None),
        check_vma=False,
    )
```

profile of v0, /device:TPU:0, one launch (start us, length us, event | category | flops | bytes accessed | tf_op | source)
XLA Modules:
  0.0 171.5 jit_solution(12089231413821765125)
XLA Ops:
  6.5 0.0 copy-start
  6.5 0.0 all-gather.2.cloned.1.call-start
  6.5 0.8 copy.24
  7.3 0.1 eq.45
  7.4 0.2 reduce_window_sum.11
  7.6 0.1 reduce_sum.30
  7.7 0.1 copy.31
  7.8 0.1 convert_reduce_fusion
  7.9 0.0 copy-done
  7.9 0.2 convolution_convert_fusion
  8.1 0.1 reshape.100
  8.2 3.8 %all_to_all.20 = bf16[2,2,4,4096]{3,2,1,0:T(4,128)(2,1)S(1)} all-to-all(bf16[2,2,4,4096]{3,2,1,0:T(4,128)(2,1)S(1)} %reshape.100), channel_id=1, replica_groups=mesh['rep'=2,'exp'=2,'tp'=8] {'exp'}, dimensions={0} | all-to-all | bytes 262144 | tf_op jit(solution)/shard_map/all_to_all | solution.py:30
  12.1 0.7 reshape.101
  12.8 0.0 all-gather.2.cloned.1.call-update
  12.8 0.0 reduce-scatter.2.cloned.1.call-start
  12.8 43.1 %all-gather.2.cloned.1.call-done = bf16[2,64,4096]{2,1,0:T(8,128)(2,1)} async-done(((bf16[2,8,4096]{2,1,0:T(8,128)(2,1)}), bf16[2,64,4096]{2,1,0:T(8,128)(2,1)}) %all-gather.2.cloned.1.call-update) | async-done | bytes 1048592 | tf_op jit(solution)/shard_map/all_gather | solution.py:32
  55.9 0.0 copy-start.2
  55.9 12.2 %fusion.16 = f32[2,64,1792]{2,1,0:T(8,128)S(1)} fusion(bf16[2,64,4096]{2,1,0:T(8,128)(2,1)} %all-gather.2.cloned.1.call-done, bf16[2,4096,1792]{2,1,0:T(8,128)(2,1)} %param.9), kind=kOutput, calls=%fused_computation.34 | convolution fusion | flops 1879048192 | bytes 31326208 | tf_op jit(solution)/shard_map/lrd,ldf->lrf/dot_general | solution.py:33
  68.1 0.0 copy-done.2
  68.1 0.0 copy-start.3
  68.1 0.0 copy-start.1
  68.1 23.1 %convolution_bitcast_fusion = f32[64,2,4096]{2,0,1:T(8,128)} fusion(bf16[2,1792,4096]{2,1,0:T(8,128)(2,1)} %param.11, bf16[2,64,4096]{2,1,0:T(8,128)(2,1)S(1)} %copy-done.2, bf16[2,4096,1792]{2,1,0:T(8,128)(2,1)} %param.10, f32[2,64,1792]{2,1,0:T(8,128)S(1)} %fusion.16), kind=kOutput, calls=%fused_computation | convolution fusion | flops 3759472640 | bytes 62783488 | tf_op jit(solution)/shard_map/lrf,lfd->rld/dot_general | solution.py:37
  91.2 0.0 reduce-scatter.2.cloned.1.call-update
  91.2 0.1 copy.29
  91.3 0.0 copy-done.3
  91.3 0.1 select_reduce_fusion
  91.4 67.1 %reduce-scatter.2.cloned.1.call-done = f32[8,2,4096]{2,0,1:T(8,128)} async-done(((f32[64,2,4096]{2,0,1:T(8,128)}), f32[8,2,4096]{2,0,1:T(8,128)}) %reduce-scatter.2.cloned.1.call-update) | async-done | bytes 262160 | tf_op jit(solution)/shard_map/reduce_scatter | solution.py:36
  158.5 1.2 copy.34
  159.7 3.9 %all_to_all.21 = f32[2,4,2,4096]{3,2,1,0:T(2,128)S(1)} all-to-all(f32[2,4,2,4096]{3,2,1,0:T(2,128)S(1)} %bitcast.15), channel_id=1, replica_groups=mesh['rep'=2,'exp'=2,'tp'=8] {'exp'}, dimensions={0} | all-to-all | bytes 524288 | tf_op jit(solution)/shard_map/all_to_all | solution.py:43
  163.6 0.2 reshape.103
  163.8 0.9 convolution_convert_fusion.1
  164.7 0.0 copy-done.1
  (5 shorter events, 0.1 us)
Async XLA Ops:
  6.5 1.4 copy-start
  6.5 49.4 %all-gather.2.cloned.1.call-start = ((), (), s32[]{:S(2)}) async-start(), calls=%async_computation.3 | async-start | bytes 1179648 | tf_op jit(solution)/shard_map/all_gather | solution.py:32
  12.8 145.8 %reduce-scatter.2.cloned.1.call-start = ((), (), s32[]{:S(2)}) async-start(), calls=%async_computation.4 | async-start | bytes 2359296 | tf_op jit(solution)/shard_map/reduce_scatter | solution.py:36
  55.9 12.2 %copy-start.2 = (bf16[2,64,4096]{2,1,0:T(8,128)(2,1)S(1)}, bf16[2,64,4096]{2,1,0:T(8,128)(2,1)}, u32[]{:S(2)}) copy-start(bf16[2,64,4096]{2,1,0:T(8,128)(2,1)} %all-gather.2.cloned.1.call-done) | copy-start | bytes 3145732
  68.1 23.2 %copy-start.3 = (s32[4,2]{0,1:T(2,128)S(1)}, s32[4,2]{0,1:T(2,128)}, u32[]{:S(2)}) copy-start(s32[4,2]{0,1:T(2,128)} %param.8) | copy-start | bytes 100
  68.1 96.6 %copy-start.1 = (bf16[4,4096]{1,0:T(4,128)(2,1)S(1)}, bf16[4,4096]{1,0:T(4,128)(2,1)}, u32[]{:S(2)}) copy-start(bf16[4,4096]{1,0:T(4,128)(2,1)} %param.6) | copy-start | bytes 98308
Sparse Core Ops, SparseCore 0:
  12.9 42.9 all-gather.1
  91.4 67.1 reduce-scatter.1
where the time goes:
time: 172 us
  waiting for transfers between devices  110 us (64%)
  matrix products  36.3 us (21%)
  between operations  13.5 us (8%)
  blocking collectives  7.78 us (5%)
  local copies, waits for them, and re-layouts  3.27 us (2%)
    reduce_scatter x1, waiting for transfers between devices, body(): lax.psum_scatter(jnp.einsum('lrf,lfd->rld', hidden, down_weight, preferre...  67.1 us
    all_gather x1, waiting for transfers between devices, body(): piece = lax.all_gather(arrived, 'tp', axis=1, tiled=True)  43.1 us
    dot_general x1, matrix products, body(): jnp.einsum('lrf,lfd->rld', hidden, down_weight, preferred_element_type=jn...  23.1 us
    dot_general x1, matrix products, body(): jnp.einsum('lrd,ldf->lrf', piece, gate_weight, preferred_element_type=jnp...  12.2 us
    all_to_all x1, blocking collectives, body(): lax.all_to_all(summed, 'exp', split_axis=0, concat_axis=0, tiled=True)  3.94 us
    all_to_all x1, blocking collectives, body(): lax.all_to_all(outgoing, 'exp', split_axis=0, concat_axis=2, tiled=True)  3.84 us
  transfers between devices with their start and end apart: 2, of which 2 were waited for; matrix products, arithmetic and copies ran while one was open for 0% of the time, Pallas kernels for 0%

commit v1 on v0

v1 whole, which is shorter than its diff:
```python
import functools

import jax
import jax.numpy as jnp
from jax import lax
from jax.experimental import pallas as pl
from jax.experimental.pallas import tpu as pltpu
from jax.sharding import PartitionSpec as P

MESH = pl.DeviceIdType.MESH
LANES = 128
VMEM_BYTES = 67043328


def kernel(
    nt, kb, cw, gu_slots, dn_slots,
    ids_ref, gates_ref, tok_ref, gw_ref, uw_ref, dw_ref, out_ref,
    xg, stage, x, wst, acc_g, acc_u, h, gu_buf, dn_buf,
    part, ex_send, ex_recv, tp_send, tp_recv,
    gu_sem, dn_sem, ga_send, ga_fwd, ga_recv, ex_ssem, ex_rsem, tp_ssem, tp_rsem,
):
    e = lax.axis_index("exp")
    t = lax.axis_index("tp")
    other = 1 - e
    me = e * nt + t
    rows, width = tok_ref.shape
    experts, _, hidden = gw_ref.shape
    tokens = x.shape[1]
    half = tokens // 2
    nk = width // kb
    nc = width // cw
    gu_steps = experts * nk

    def gu_copies(i, slot):
        l = i // nk
        k0 = pl.multiple_of((i % nk) * kb, kb)
        return [
            pltpu.make_async_copy(
                ref.at[l, pl.ds(k0, kb), :], gu_buf.at[slot, m], gu_sem.at[slot, m]
            )
            for m, ref in enumerate((gw_ref, uw_ref))
        ]

    def dn_copies(c, slot):
        c0 = pl.multiple_of(c * cw, cw)
        return [
            pltpu.make_async_copy(
                dw_ref.at[l, :, pl.ds(c0, cw)], dn_buf.at[slot, l], dn_sem.at[slot, l]
            )
            for l in range(experts)
        ]

    def first(i, carry):
        for copy in gu_copies(i, i):
            copy.start()
        return carry

    lax.fori_loop(0, gu_slots, first, 0)

    barrier = pltpu.get_barrier_semaphore()

    def greet(d, carry):
        pl.semaphore_signal(
            barrier, inc=1, device_id={"tp": (t + d) % nt}, device_id_type=MESH
        )
        return carry

    lax.fori_loop(1, nt, greet, 0)
    pl.semaphore_signal(barrier, inc=1, device_id={"exp": other}, device_id_type=MESH)

    lane = lax.broadcasted_iota(jnp.int32, (rows, LANES), 1)
    sub = lax.broadcasted_iota(jnp.int32, (rows, LANES), 0)
    weight = jnp.zeros((rows, LANES), jnp.float32)
    for r in range(rows):
        for k in range(ids_ref.shape[0]):
            value = gates_ref[k, r].astype(jnp.float32) * (1.0 / 256.0)
            weight += jnp.where((sub == r) & (lane == ids_ref[k, r]), value, 0.0)
    xg[me, :, :width] = tok_ref[...]
    xg[me, :, width:] = weight.astype(jnp.bfloat16)

    pl.semaphore_wait(barrier, nt)

    def to_other(tt):
        slot = e * nt + tt
        return pltpu.make_async_remote_copy(
            src_ref=xg.at[slot], dst_ref=xg.at[slot],
            send_sem=ga_fwd.at[tt], recv_sem=ga_recv.at[slot],
            device_id={"exp": other}, device_id_type=MESH,
        )

    def to_tp(d):
        return pltpu.make_async_remote_copy(
            src_ref=xg.at[me], dst_ref=xg.at[me],
            send_sem=ga_send.at[d], recv_sem=ga_recv.at[me],
            device_id={"tp": (t + d) % nt}, device_id_type=MESH,
        )

    def from_slot(slot):
        return pltpu.make_async_remote_copy(
            src_ref=xg.at[slot], dst_ref=xg.at[slot],
            send_sem=ga_send.at[0], recv_sem=ga_recv.at[slot],
            device_id={"exp": other}, device_id_type=MESH,
        )

    def push(d, carry):
        to_tp(d).start()
        return carry

    lax.fori_loop(1, nt, push, 0)
    to_other(t).start()

    def relay(d, carry):
        source = (t + nt - d) % nt
        from_slot(e * nt + source).wait_recv()
        to_other(source).start()
        return carry

    lax.fori_loop(1, nt, relay, 0)

    def arrive(tt, carry):
        from_slot(other * nt + tt).wait_recv()
        return carry

    lax.fori_loop(0, nt, arrive, 0)

    group = stage.shape[0] // rows

    def lay(g, carry):
        for i in range(group):
            stage[i * rows:(i + 1) * rows, :] = xg[g * group + i].astype(jnp.float32)
        r0 = pl.multiple_of(g * group * rows, group * rows)
        for k in range(nk):
            x[k, pl.ds(r0, group * rows), :] = stage[:, k * kb:(k + 1) * kb].astype(jnp.bfloat16)
        wst[pl.ds(r0, group * rows), :] = stage[:, width:]
        return carry

    lax.fori_loop(0, tokens // (group * rows), lay, 0)

    tiles = [(n, min(256, hidden - n)) for n in range(0, hidden, 256)]

    def gu_step(i, carry):
        slot = i % gu_slots
        k = i % nk
        for copy in gu_copies(i, slot):
            copy.wait()

        @pl.when(k == 0)
        def _():
            acc_g[...] = jnp.zeros_like(acc_g)
            acc_u[...] = jnp.zeros_like(acc_u)

        xk = x[k]
        for n, size in tiles:
            for m, acc in enumerate((acc_g, acc_u)):
                acc[:, n:n + size] += jnp.dot(
                    xk, gu_buf[slot, m, :, n:n + size], preferred_element_type=jnp.float32
                )

        @pl.when(k == nk - 1)
        def _():
            for n, size in tiles:
                gate = acc_g[:, n:n + size]
                silu = gate / (1.0 + jnp.exp(-gate))
                h[i // nk, :, n:n + size] = (silu * acc_u[:, n:n + size]).astype(jnp.bfloat16)

        later = i + gu_slots

        @pl.when(later < gu_steps)
        def _():
            for copy in gu_copies(later, slot):
                copy.start()

        column = later - gu_steps

        @pl.when((column >= 0) & (column < dn_slots))
        def _():
            for copy in dn_copies(column, column):
                copy.start()

        return carry

    lax.fori_loop(0, gu_steps, gu_step, 0)

    lanes = lax.broadcasted_iota(jnp.int32, (tokens, LANES), 1)
    scales = [
        jnp.sum(jnp.where(lanes == e * experts + l, wst[...], 0.0), axis=1, keepdims=True)
        for l in range(experts)
    ]

    def ex_copy(c):
        return pltpu.make_async_remote_copy(
            src_ref=ex_send.at[c], dst_ref=ex_recv.at[c],
            send_sem=ex_ssem.at[c], recv_sem=ex_rsem.at[c],
            device_id={"exp": other}, device_id_type=MESH,
        )

    def tp_copy(c, d):
        target = (t + d) % nt
        return pltpu.make_async_remote_copy(
            src_ref=tp_send.at[c, target], dst_ref=tp_recv.at[c, t],
            send_sem=tp_ssem.at[c, d], recv_sem=tp_rsem.at[c, t],
            device_id={"tp": target}, device_id_type=MESH,
        )

    def tp_from(c, source):
        return pltpu.make_async_remote_copy(
            src_ref=tp_send.at[c, source], dst_ref=tp_recv.at[c, source],
            send_sem=tp_ssem.at[c, 0], recv_sem=tp_rsem.at[c, source],
            device_id={"tp": source}, device_id_type=MESH,
        )

    def pass_on(c):
        ex_copy(c).wait_recv()
        total = part[c, e] + ex_recv[c].astype(jnp.float32)
        for j in range(nt):
            tp_send[c, j] = total[j * rows:(j + 1) * rows, :].astype(jnp.bfloat16)
        tp_recv[c, t] = tp_send[c, t]

        def send(d, carry):
            tp_copy(c, d).start()
            return carry

        lax.fori_loop(1, nt, send, 0)

    def dn_step(c, carry):
        slot = c % dn_slots
        for copy in dn_copies(c, slot):
            copy.wait()
        for n in range(0, cw, 256):
            size = min(256, cw - n)
            total = jnp.zeros((tokens, size), jnp.float32)
            for l in range(experts):
                total += scales[l] * jnp.dot(
                    h[l], dn_buf[slot, l, :, n:n + size], preferred_element_type=jnp.float32
                )
            part[c, 0, :, n:n + size] = total[:half]
            part[c, 1, :, n:n + size] = total[half:]
        ex_send[c] = part[c, other].astype(jnp.bfloat16)
        ex_copy(c).start()
        later = c + dn_slots

        @pl.when(later < nc)
        def _():
            for copy in dn_copies(later, slot):
                copy.start()

        @pl.when(c > 0)
        def _():
            pass_on(c - 1)

        return carry

    lax.fori_loop(0, nc, dn_step, 0)
    pass_on(nc - 1)

    for c in range(nc):
        def collect(d, carry, c=c):
            tp_from(c, (t + nt - d) % nt).wait_recv()
            return carry

        lax.fori_loop(1, nt, collect, 0)
        total = tp_recv[c, 0].astype(jnp.float32)
        for j in range(1, nt):
            total += tp_recv[c, j].astype(jnp.float32)
        out_ref[:, c * cw:(c + 1) * cw] = total.astype(out_ref.dtype)

    def finish(d, carry):
        to_tp(d).wait_send()
        to_other((t + d) % nt).wait_send()

        def drain(c, inner):
            tp_copy(c, d).wait_send()
            return inner

        lax.fori_loop(0, nc, drain, 0)
        return carry

    lax.fori_loop(1, nt, finish, 0)
    to_other(t).wait_send()

    def drain_ex(c, carry):
        ex_copy(c).wait_send()
        return carry

    lax.fori_loop(0, nc, drain_ex, 0)


def body(tokens, expert_ids, gate_ints, gate_weight, up_weight, down_weight):
    rows, width = tokens.shape
    experts, _, hidden = gate_weight.shape
    nt = lax.axis_size("tp")
    slots = nt * lax.axis_size("exp")
    total = slots * rows
    kb = min(512, width)
    cw = min(512, width)
    nk, nc = width // kb, width // cw
    gu_slots = min(12, experts * nk)
    dn_slots = min(4, nc)
    bf16, f32 = jnp.bfloat16, jnp.float32
    vmem = pl.BlockSpec(memory_space=pltpu.VMEM)
    smem = pl.BlockSpec(memory_space=pltpu.SMEM)
    hbm = pl.BlockSpec(memory_space=pl.ANY)
    dma = pltpu.SemaphoreType.DMA
    return pl.pallas_call(
        functools.partial(kernel, nt, kb, cw, gu_slots, dn_slots),
        out_shape=jax.ShapeDtypeStruct((rows, width), bf16),
        in_specs=[smem, smem, vmem, hbm, hbm, hbm],
        out_specs=vmem,
        scratch_shapes=[
            pltpu.VMEM((slots, rows, width + LANES), bf16),
            pltpu.VMEM((16, width + LANES), f32),
            pltpu.VMEM((nk, total, kb), bf16),
            pltpu.VMEM((total, LANES), f32),
            pltpu.VMEM((total, hidden), f32),
            pltpu.VMEM((total, hidden), f32),
            pltpu.VMEM((experts, total, hidden), bf16),
            pltpu.VMEM((gu_slots, 2, kb, hidden), bf16),
            pltpu.VMEM((dn_slots, experts, hidden, cw), bf16),
            pltpu.VMEM((nc, 2, total // 2, cw), f32),
            pltpu.VMEM((nc, total // 2, cw), bf16),
            pltpu.VMEM((nc, total // 2, cw), bf16),
            pltpu.VMEM((nc, nt, rows, cw), bf16),
            pltpu.VMEM((nc, nt, rows, cw), bf16),
            dma((gu_slots, 2)),
            dma((dn_slots, experts)),
            dma((nt,)),
            dma((nt,)),
            dma((slots,)),
            dma((nc,)),
            dma((nc,)),
            dma((nc, nt)),
            dma((nc, nt)),
        ],
        compiler_params=pltpu.CompilerParams(
            collective_id=0, has_side_effects=True, vmem_limit_bytes=VMEM_BYTES
        ),
    )(expert_ids.T, gate_ints.T, tokens, gate_weight, up_weight, down_weight)


def solution(mesh):
    return jax.shard_map(
        body,
        mesh=mesh,
        in_specs=(
            P(("rep", "exp", "tp"), None),
            P(("rep", "exp", "tp"), None),
            P(("rep", "exp", "tp"), None),
            P("exp", None, "tp"),
            P("exp", None, "tp"),
            P("exp", "tp", None),
        ),
        out_specs=P(("rep", "exp", "tp"), None),
        check_vma=False,
    )
```

time: 172 us -> 46 us (0.27)
  waiting for transfers between devices: 110 us -> 0 us
  Pallas kernels: 0 us -> 44.4 us
  matrix products: 36.3 us -> 0 us
  between operations: 13.5 us -> 0.01 us
  blocking collectives: 7.78 us -> 0 us
  local copies, waits for them, and re-layouts: 3.27 us -> 1.39 us
    reduce_scatter x1 -> x0, waiting for transfers between devices: 67.1 us -> none  [body(): lax.psum_scatter(jnp.einsum('lrf,lfd->rld', hidden, down_weight, preferre...]
    pallas_call x0 -> x1, Pallas kernels: none -> 44.4 us  [body(): pl.pallas_call(functools.partial(kernel, nt, kb, cw, gu_slots, dn_slots),...]
    all_gather x1 -> x0, waiting for transfers between devices: 43.1 us -> none  [body(): piece = lax.all_gather(arrived, 'tp', axis=1, tiled=True)]
    dot_general x4 -> x0, matrix products: 36.3 us -> none  [the longest x1 23.1 us: body(): jnp.einsum('lrf,lfd->rld', hidden, down_weight, preferred_element_type=jn...]
    all_to_all x2 -> x0, blocking collectives: 7.78 us -> none  [the longest x1 3.94 us: body(): lax.all_to_all(summed, 'exp', split_axis=0, concat_axis=0, tiled=True)]
    reshape x4 -> x0, local copies, waits for them, and re-layouts: 2.07 us -> none  [the longest x1 1.15 us: body(): summed = summed.reshape(groups, tok_rows, local_experts, width)]
  transfers between devices with their start and end apart: 2 -> 0, of which waited for: 2 -> 0; matrix products, arithmetic and copies ran while one was open for 0% -> 0% of each run, Pallas kernels for 0% -> 0%
where the time goes in v1:
time: 46 us; the launch traced here: 45.8 us
  Pallas kernels  44.4 us (97%)
  local copies, waits for them, and re-layouts  1.39 us (3%)
    pallas_call x1, Pallas kernels, body(): pl.pallas_call(functools.partial(kernel, nt, kb, cw, gu_slots, dn_slots),...  44.4 us
    unnamed x1, local copies, waits for them, and re-layouts  1.39 us

profile of v1, /device:TPU:0, one launch (start us, length us, event | category | flops | bytes accessed | tf_op | source)
XLA Modules:
  0.0 45.8 jit_solution(12343269916954171651)
XLA Ops:
  0.0 44.4 %shard_map.64 = bf16[4,4096]{1,0:T(4,128)(2,1)} custom-call(s32[2,4]{1,0:T(2,128)} %bitcast.2, s32[2,4]{1,0:T(2,128)} %bitcast.3, bf16[4,4096]{1,0:T(4,128)(2,1)} %tok_ref.1, bf16[2,4096,1792]{2,1,0:T(8,128)(2,1)} %gw_ref.1, bf16[2,4096,1792]{2,1,0:T(8,128)(2,1)} %uw_ref.1, bf16[2,1792,4096]{2,1,0:T(8,128)(2,1)} %dw_ref.1), custom_call_target="tpu_custom_call" | custom-call | tf_op jit(solution)/shard_map/pallas_call | solution.py:304
  44.4 1.4 %copy.8 = bf16[4,4096]{1,0:T(4,128)(2,1)} copy(bf16[4,4096]{1,0:T(4,128)(2,1)} %shard_map.64) | data formatting | bytes 65536

commit v2 on v1

--- a/solution.py
+++ b/solution.py
@@ -13,9 +13,9 @@
 
 
 def kernel(
-    nt, kb, cw, gu_slots, dn_slots,
+    nt, fb, cw, gu_slots, dn_slots,
     ids_ref, gates_ref, tok_ref, gw_ref, uw_ref, dw_ref, out_ref,
-    xg, stage, x, wst, acc_g, acc_u, h, gu_buf, dn_buf,
+    xg, stage, x, wst, h, gu_buf, dn_buf,
     part, ex_send, ex_recv, tp_send, tp_recv,
     gu_sem, dn_sem, ga_send, ga_fwd, ga_recv, ex_ssem, ex_rsem, tp_ssem, tp_rsem,
 ):
@@ -25,18 +25,18 @@
     me = e * nt + t
     rows, width = tok_ref.shape
     experts, _, hidden = gw_ref.shape
-    tokens = x.shape[1]
+    tokens = x.shape[0]
     half = tokens // 2
-    nk = width // kb
+    nf = hidden // fb
     nc = width // cw
-    gu_steps = experts * nk
+    gu_steps = experts * nf
 
     def gu_copies(i, slot):
-        l = i // nk
-        k0 = pl.multiple_of((i % nk) * kb, kb)
+        l = i // nf
+        columns = pl.ds(pl.multiple_of((i % nf) * fb, fb), fb) if nf > 1 else slice(None)
         return [
             pltpu.make_async_copy(
-                ref.at[l, pl.ds(k0, kb), :], gu_buf.at[slot, m], gu_sem.at[slot, m]
+                ref.at[l, :, columns], gu_buf.at[slot, m], gu_sem.at[slot, m]
             )
             for m, ref in enumerate((gw_ref, uw_ref))
         ]
@@ -129,40 +129,21 @@
         for i in range(group):
             stage[i * rows:(i + 1) * rows, :] = xg[g * group + i].astype(jnp.float32)
         r0 = pl.multiple_of(g * group * rows, group * rows)
-        for k in range(nk):
-            x[k, pl.ds(r0, group * rows), :] = stage[:, k * kb:(k + 1) * kb].astype(jnp.bfloat16)
+        x[pl.ds(r0, group * rows), :] = stage[:, :width].astype(jnp.bfloat16)
         wst[pl.ds(r0, group * rows), :] = stage[:, width:]
         return carry
 
     lax.fori_loop(0, tokens // (group * rows), lay, 0)
-
-    tiles = [(n, min(256, hidden - n)) for n in range(0, hidden, 256)]
 
     def gu_step(i, carry):
         slot = i % gu_slots
-        k = i % nk
         for copy in gu_copies(i, slot):
             copy.wait()
-
-        @pl.when(k == 0)
-        def _():
-            acc_g[...] = jnp.zeros_like(acc_g)
-            acc_u[...] = jnp.zeros_like(acc_u)
-
-        xk = x[k]
-        for n, size in tiles:
-            for m, acc in enumerate((acc_g, acc_u)):
-                acc[:, n:n + size] += jnp.dot(
-                    xk, gu_buf[slot, m, :, n:n + size], preferred_element_type=jnp.float32
-                )
-
-        @pl.when(k == nk - 1)
-        def _():
-            for n, size in tiles:
-                gate = acc_g[:, n:n + size]
-                silu = gate / (1.0 + jnp.exp(-gate))
-                h[i // nk, :, n:n + size] = (silu * acc_u[:, n:n + size]).astype(jnp.bfloat16)
-
+        gate, upper = (
+            jnp.dot(x[...], gu_buf[slot, m], preferred_element_type=jnp.float32) for m in range(2)
+        )
+        columns = pl.ds(pl.multiple_of((i % nf) * fb, fb), fb) if nf > 1 else slice(None)
+        h[i // nf, :, columns] = (gate / (1.0 + jnp.exp(-gate)) * upper).astype(jnp.bfloat16)
         later = i + gu_slots
 
         @pl.when(later < gu_steps)
@@ -291,10 +272,10 @@
     nt = lax.axis_size("tp")
     slots = nt * lax.axis_size("exp")
     total = slots * rows
-    kb = min(512, width)
+    fb = 256 if hidden % 256 == 0 else hidden
     cw = min(512, width)
-    nk, nc = width // kb, width // cw
-    gu_slots = min(12, experts * nk)
+    nf, nc = hidden // fb, width // cw
+    gu_slots = min(10, experts * nf)
     dn_slots = min(4, nc)
     bf16, f32 = jnp.bfloat16, jnp.float32
     vmem = pl.BlockSpec(memory_space=pltpu.VMEM)
@@ -302,19 +283,17 @@
     hbm = pl.BlockSpec(memory_space=pl.ANY)
     dma = pltpu.SemaphoreType.DMA
     return pl.pallas_call(
-        functools.partial(kernel, nt, kb, cw, gu_slots, dn_slots),
+        functools.partial(kernel, nt, fb, cw, gu_slots, dn_slots),
         out_shape=jax.ShapeDtypeStruct((rows, width), bf16),
         in_specs=[smem, smem, vmem, hbm, hbm, hbm],
         out_specs=vmem,
         scratch_shapes=[
             pltpu.VMEM((slots, rows, width + LANES), bf16),
             pltpu.VMEM((16, width + LANES), f32),
-            pltpu.VMEM((nk, total, kb), bf16),
+            pltpu.VMEM((total, width), bf16),
             pltpu.VMEM((total, LANES), f32),
-            pltpu.VMEM((total, hidden), f32),
-            pltpu.VMEM((total, hidden), f32),
             pltpu.VMEM((experts, total, hidden), bf16),
-            pltpu.VMEM((gu_slots, 2, kb, hidden), bf16),
+            pltpu.VMEM((gu_slots, 2, width, fb), bf16),
             pltpu.VMEM((dn_slots, experts, hidden, cw), bf16),
             pltpu.VMEM((nc, 2, total // 2, cw), f32),
             pltpu.VMEM((nc, total // 2, cw), bf16),

time: 46 us -> 45.1 us (0.980)
  Pallas kernels: 44.4 us -> 43.5 us
    pallas_call x1, Pallas kernels: 44.4 us -> 43.5 us  [body(): pl.pallas_call(functools.partial(kernel, nt, fb, cw, gu_slots, dn_slots),...]
where the time goes in v2:
time: 45.1 us; the launch traced here: 44.9 us
  Pallas kernels  43.5 us (96%)
  local copies, waits for them, and re-layouts  1.39 us (3%)
    pallas_call x1, Pallas kernels, body(): pl.pallas_call(functools.partial(kernel, nt, fb, cw, gu_slots, dn_slots),...  43.5 us
    unnamed x1, local copies, waits for them, and re-layouts  1.39 us

profile of v2, /device:TPU:0, one launch (start us, length us, event | category | flops | bytes accessed | tf_op | source)
XLA Modules:
  0.0 44.9 jit_solution(9605549560128757647)
XLA Ops:
  0.0 43.5 %shard_map.64 = bf16[4,4096]{1,0:T(4,128)(2,1)} custom-call(s32[2,4]{1,0:T(2,128)} %bitcast.2, s32[2,4]{1,0:T(2,128)} %bitcast.3, bf16[4,4096]{1,0:T(4,128)(2,1)} %tok_ref.1, bf16[2,4096,1792]{2,1,0:T(8,128)(2,1)} %gw_ref.1, bf16[2,4096,1792]{2,1,0:T(8,128)(2,1)} %uw_ref.1, bf16[2,1792,4096]{2,1,0:T(8,128)(2,1)} %dw_ref.1), custom_call_target="tpu_custom_call" | custom-call | tf_op jit(solution)/shard_map/pallas_call | solution.py:285
  43.5 1.4 %copy.8 = bf16[4,4096]{1,0:T(4,128)(2,1)} copy(bf16[4,4096]{1,0:T(4,128)(2,1)} %shard_map.64) | data formatting | bytes 65536

commit v3 on v2

--- a/solution.py
+++ b/solution.py
@@ -275,8 +275,8 @@
     fb = 256 if hidden % 256 == 0 else hidden
     cw = min(512, width)
     nf, nc = hidden // fb, width // cw
-    gu_slots = min(10, experts * nf)
-    dn_slots = min(4, nc)
+    gu_slots = min(8, experts * nf)
+    dn_slots = min(7, nc)
     bf16, f32 = jnp.bfloat16, jnp.float32
     vmem = pl.BlockSpec(memory_space=pltpu.VMEM)
     smem = pl.BlockSpec(memory_space=pltpu.SMEM)

time: 45.1 us -> 45.1 us (level)
  no operation moved by 1% of the time
where the time goes in v3:
time: 45.1 us; the launch traced here: 44.9 us
  Pallas kernels  43.5 us (96%)
  local copies, waits for them, and re-layouts  1.39 us (3%)
    pallas_call x1, Pallas kernels, body(): pl.pallas_call(functools.partial(kernel, nt, fb, cw, gu_slots, dn_slots),...  43.5 us
    unnamed x1, local copies, waits for them, and re-layouts  1.39 us

profile of v3, /device:TPU:0, one launch (start us, length us, event | category | flops | bytes accessed | tf_op | source)
XLA Modules:
  0.0 44.9 jit_solution(17332515548030766312)
XLA Ops:
  0.0 43.5 %shard_map.64 = bf16[4,4096]{1,0:T(4,128)(2,1)} custom-call(s32[2,4]{1,0:T(2,128)} %bitcast.2, s32[2,4]{1,0:T(2,128)} %bitcast.3, bf16[4,4096]{1,0:T(4,128)(2,1)} %tok_ref.1, bf16[2,4096,1792]{2,1,0:T(8,128)(2,1)} %gw_ref.1, bf16[2,4096,1792]{2,1,0:T(8,128)(2,1)} %uw_ref.1, bf16[2,1792,4096]{2,1,0:T(8,128)(2,1)} %dw_ref.1), custom_call_target="tpu_custom_call" | custom-call | tf_op jit(solution)/shard_map/pallas_call | solution.py:285
  43.5 1.4 %copy.8 = bf16[4,4096]{1,0:T(4,128)(2,1)} copy(bf16[4,4096]{1,0:T(4,128)(2,1)} %shard_map.64) | data formatting | bytes 65536

commit v4 on v3

--- a/solution.py
+++ b/solution.py
@@ -23,6 +23,8 @@
     t = lax.axis_index("tp")
     other = 1 - e
     me = e * nt + t
+    pair = t + 1 - 2 * (t % 2)
+    same = nt // 2
     rows, width = tok_ref.shape
     experts, _, hidden = gw_ref.shape
     tokens = x.shape[0]
@@ -92,7 +94,15 @@
         return pltpu.make_async_remote_copy(
             src_ref=xg.at[me], dst_ref=xg.at[me],
             send_sem=ga_send.at[d], recv_sem=ga_recv.at[me],
-            device_id={"tp": (t + d) % nt}, device_id_type=MESH,
+            device_id={"tp": (t + 2 * d) % nt}, device_id_type=MESH,
+        )
+
+    def to_pair(d):
+        slot = e * nt + (t + nt - 2 * d) % nt
+        return pltpu.make_async_remote_copy(
+            src_ref=xg.at[slot], dst_ref=xg.at[slot],
+            send_sem=ga_send.at[same + d], recv_sem=ga_recv.at[slot],
+            device_id={"tp": pair}, device_id_type=MESH,
         )
 
     def from_slot(slot):
@@ -106,16 +116,26 @@
         to_tp(d).start()
         return carry
 
-    lax.fori_loop(1, nt, push, 0)
+    lax.fori_loop(1, same, push, 0)
+    to_pair(0).start()
     to_other(t).start()
 
     def relay(d, carry):
-        source = (t + nt - d) % nt
+        source = (t + nt - 2 * d) % nt
+        from_slot(e * nt + source).wait_recv()
+        to_pair(d).start()
+        to_other(source).start()
+        return carry
+
+    lax.fori_loop(1, same, relay, 0)
+
+    def hand_over(d, carry):
+        source = (pair + nt - 2 * d) % nt
         from_slot(e * nt + source).wait_recv()
         to_other(source).start()
         return carry
 
-    lax.fori_loop(1, nt, relay, 0)
+    lax.fori_loop(0, same, hand_over, 0)
 
     def arrive(tt, carry):
         from_slot(other * nt + tt).wait_recv()
@@ -246,7 +266,6 @@
         out_ref[:, c * cw:(c + 1) * cw] = total.astype(out_ref.dtype)
 
     def finish(d, carry):
-        to_tp(d).wait_send()
         to_other((t + d) % nt).wait_send()
 
         def drain(c, inner):
@@ -258,6 +277,14 @@
 
     lax.fori_loop(1, nt, finish, 0)
     to_other(t).wait_send()
+    to_pair(0).wait_send()
+
+    def finish_gather(d, carry):
+        to_tp(d).wait_send()
+        to_pair(d).wait_send()
+        return carry
+
+    lax.fori_loop(1, same, finish_gather, 0)
 
     def drain_ex(c, carry):
         ex_copy(c).wait_send()

time: 45.1 us -> 45.4 us (level)
  no operation moved by 1% of the time
where the time goes in v4:
time: 45.4 us; the launch traced here: 45.1 us
  Pallas kernels  43.7 us (96%)
  local copies, waits for them, and re-layouts  1.39 us (3%)
    pallas_call x1, Pallas kernels, body(): pl.pallas_call(functools.partial(kernel, nt, fb, cw, gu_slots, dn_slots),...  43.7 us
    unnamed x1, local copies, waits for them, and re-layouts  1.39 us

profile of v4, /device:TPU:0, one launch (start us, length us, event | category | flops | bytes accessed | tf_op | source)
XLA Modules:
  0.0 45.1 jit_solution(15726176175757450605)
XLA Ops:
  0.0 43.7 %shard_map.64 = bf16[4,4096]{1,0:T(4,128)(2,1)} custom-call(s32[2,4]{1,0:T(2,128)} %bitcast.2, s32[2,4]{1,0:T(2,128)} %bitcast.3, bf16[4,4096]{1,0:T(4,128)(2,1)} %tok_ref.1, bf16[2,4096,1792]{2,1,0:T(8,128)(2,1)} %gw_ref.1, bf16[2,4096,1792]{2,1,0:T(8,128)(2,1)} %uw_ref.1, bf16[2,1792,4096]{2,1,0:T(8,128)(2,1)} %dw_ref.1), custom_call_target="tpu_custom_call" | custom-call | tf_op jit(solution)/shard_map/pallas_call | solution.py:312
  43.7 1.4 %copy.8 = bf16[4,4096]{1,0:T(4,128)(2,1)} copy(bf16[4,4096]{1,0:T(4,128)(2,1)} %shard_map.64) | data formatting | bytes 65536
